TPU v7x, 32 devices: a whole 2x2x4 slice. The times are simulated.
32 devices in a mesh: depth: 2 (over x), map: 16 (over z, y, core).
Axes of the slice: x: 2, y: 2, z: 4, core: 2. Of those that a mesh axis runs over, the one named last changes fastest.
Arguments:
- velocity: float32 [3, 32, 512, 128], P(None, 'depth', 'map'), may hold values from -6 to 6
- stress: float32 [6, 32, 512, 128], P(None, 'depth', 'map'), may hold values from -6 to 6
- region: int32 [32, 512, 128], P('depth', 'map'), may hold values from 0 to 7
- lame_table: float32 [8], replicated, may hold values from 0.2 to 0.5
- shear_table: float32 [8], replicated, may hold values from 0.1 to 0.3
- buoyancy_table: float32 [8], replicated, may hold values from 0.6 to 1.2
- height: float32 [256, 4096], P('depth', 'map'), may hold values from -6 to 6
- discharge: float32 [2, 256, 4096], P(None, 'depth', 'map'), may hold values from -6 to 6
- face_depth: float32 [2, 256, 4096], P(None, 'depth', 'map'), may hold values from 0.5 to 2
- wet: int32 [256, 4096], P('depth', 'map'), may hold values 0 or 1
- seafloor_index: int32 [256, 4096], P('depth', 'map'), may hold values from 0 to 4095
Outputs:
- velocity_out: float32 [3, 32, 512, 128], P(None, 'depth', 'map')
- stress_out: float32 [6, 32, 512, 128], P(None, 'depth', 'map')
- height_out: float32 [256, 4096], P('depth', 'map')
- discharge_out: float32 [2, 256, 4096], P(None, 'depth', 'map')
Inputs may be any that keep to these rules, and one draw needn't show every extreme that they name: `wet`: 1 for a wet ocean cell, 0 for a dry one. `seafloor_index`: index k of the seafloor cell under an ocean cell, among the 32 x 128 crust cells of its own map column, counted row by row.
All inputs are finite; a program needn't handle non-finite values. No bound on the sum of `wet` on one device may be relied on, other than what follows from the above.
Results may differ from a plain program's by a relative error of at most 0.000054.
Values sent between devices are 32-bit elements; how exact they have to be, the bound alone decides.
No kernel may reach another device: no remote copies, remote signals or barrier semaphores. Data moves between devices by JAX's collectives and lax.ppermute only.
A program may use at most 64 MiB of HBM per device.

v0:
```python
import math
import jax
import jax.numpy as jnp
from jax import lax
from jax.sharding import PartitionSpec as P

ITERS = 3
OSTEPS = 2
near_coef = 9.0 / 8.0
far_coef = 1.0 / 24.0
time_step = 0.2
ocean_step = 0.2
gravity = 1.0


def extended(x, sides, width):
    for axis, dim in sides:
        peers, length = (lax.axis_size(axis), x.shape[dim])
        up = [(i, (i + 1) % peers) for i in range(peers - 1)]
        down = [(j, i) for i, j in up]
        last = lax.slice_in_dim(x, length - width, length, axis=dim)
        leading = lax.slice_in_dim(x, 0, width, axis=dim)
        before = lax.ppermute(last, axis, up)
        after = lax.ppermute(leading, axis, down)
        x = jnp.concatenate([before, x, after], axis=dim)
    return x


def broadcast(x, axis, root):
    mine = lax.axis_index(axis) == root
    return lax.psum(jnp.where(mine, x, jnp.zeros_like(x)), axis)


def passed_along(x, axis, by):
    peers = lax.axis_size(axis)
    pairs = [(i, i + by) for i in range(peers) if 0 <= i + by < peers]
    return lax.ppermute(x, axis, pairs)


def cells(padded, axis, offset, count):
    return lax.slice_in_dim(padded, offset, offset + count, axis=axis)


def forward_diff(padded, axis):
    count = padded.shape[axis] - 4
    return near_coef * (
        cells(padded, axis, 3, count) - cells(padded, axis, 2, count)
    ) - far_coef * (cells(padded, axis, 4, count) - cells(padded, axis, 1, count))


def backward_diff(padded, axis):
    count = padded.shape[axis] - 4
    return near_coef * (
        cells(padded, axis, 2, count) - cells(padded, axis, 1, count)
    ) - far_coef * (cells(padded, axis, 3, count) - cells(padded, axis, 0, count))


def forward_y(field):
    return near_coef * (jnp.roll(field, -1, 2) - field) - far_coef * (
        jnp.roll(field, -2, 2) - jnp.roll(field, 1, 2)
    )


def backward_y(field):
    return near_coef * (field - jnp.roll(field, 1, 2)) - far_coef * (
        jnp.roll(field, -1, 2) - jnp.roll(field, 2, 2)
    )


def lookup(region, table):
    total = jnp.zeros(region.shape, jnp.float32)
    for value in range(table.shape[0]):
        total = total + jnp.where(region == value, table[value], 0.0)
    return total


def seafloor_pick(tiles, seafloor_index):
    tile_rows = tiles.shape[1]
    tile_cols = tiles.shape[2]
    ocean_rows = seafloor_index.shape[0]
    ocean_cols = seafloor_index.shape[1]
    group = math.gcd(ocean_rows, 8)
    table = jnp.transpose(tiles, (1, 0, 2)).reshape(tile_rows, 2 * tile_cols)
    row_ids = lax.broadcasted_iota(jnp.int32, (1, 1, tile_rows), 2)
    col_ids = lax.broadcasted_iota(jnp.int32, (1, 1, tile_cols), 2)

    def one_block(indices):
        upper = indices // tile_cols
        lower = indices % tile_cols
        onehot = (upper[:, :, None] == row_ids).astype(jnp.float32)
        picked = jnp.einsum("rck,kn->rcn", onehot, table, precision=lax.Precision.HIGHEST)
        chosen = lower[:, :, None] == col_ids
        first = jnp.sum(jnp.where(chosen, picked[:, :, :tile_cols], 0.0), axis=2)
        second = jnp.sum(jnp.where(chosen, picked[:, :, tile_cols:], 0.0), axis=2)
        return jnp.stack([first, second])

    blocks = seafloor_index.reshape(ocean_rows // group, group, ocean_cols)
    result = lax.map(one_block, blocks)
    result = jnp.transpose(result, (1, 0, 2, 3)).reshape(2, ocean_rows, ocean_cols)
    return (result[0], result[1])


def per_device(
    velocity,
    stress,
    region,
    lame_table,
    shear_table,
    buoyancy_table,
    height,
    discharge,
    face_depth,
    wet,
    seafloor_index,
):
    lame = lookup(region, lame_table)
    shear = lookup(region, shear_table)
    buoyancy = lookup(region, buoyancy_table)
    speeds = velocity
    forces = stress
    lift = jnp.zeros((velocity.shape[2], velocity.shape[3]), jnp.float32)
    for turn in range(ITERS):
        map_part = extended(forces[0:3], (("map", 2),), 2)
        depth_part = extended(forces[2:5], (("depth", 1),), 2)
        speed_x = speeds[0] + time_step * buoyancy * (
            forward_diff(map_part[0], 1) + backward_y(forces[1]) + backward_diff(depth_part[0], 0)
        )
        speed_y = speeds[1] + time_step * buoyancy * (
            backward_diff(map_part[1], 1) + forward_y(forces[5]) + backward_diff(depth_part[1], 0)
        )
        speed_z = speeds[2] + time_step * buoyancy * (
            backward_diff(map_part[2], 1) + backward_y(forces[3]) + forward_diff(depth_part[2], 0)
        )
        speeds = jnp.stack([speed_x, speed_y, speed_z])
        lift = lift + time_step * speed_z[0]
        beside_all = extended(speeds, (("depth", 1), ("map", 2)), 2)
        speed_map = beside_all[:, 2:-2]
        speed_depth = beside_all[:, :, 2:-2]
        strain_x = backward_diff(speed_map[0], 1)
        strain_y = backward_y(speed_y)
        strain_z = backward_diff(speed_depth[2], 0)
        spread = strain_x + strain_y + strain_z
        forces = jnp.stack(
            [
                forces[0] + time_step * (lame * spread + 2.0 * shear * strain_x),
                forces[1]
                + time_step * shear * (forward_y(speed_x) + forward_diff(speed_map[1], 1)),
                forces[2]
                + time_step
                * shear
                * (forward_diff(speed_depth[0], 0) + forward_diff(speed_map[2], 1)),
                forces[3]
                + time_step * shear * (forward_diff(speed_depth[1], 0) + forward_y(speed_z)),
                forces[4] + time_step * (lame * spread + 2.0 * shear * strain_z),
                forces[5] + time_step * (lame * spread + 2.0 * shear * strain_y),
            ]
        )
    tiles = broadcast(jnp.stack([lift, speeds[2][0]]), "depth", 0)
    lift_at, rate_at = seafloor_pick(tiles, seafloor_index)
    wetness = wet.astype(jnp.float32)
    level = wetness * (height + lift_at)
    source = wetness * rate_at
    east_pair = passed_along(jnp.stack([level[:, :1], wetness[:, :1]]), "map", -1)
    north_pair = passed_along(jnp.stack([level[:1, :], wetness[:1, :]]), "depth", -1)
    wet_east = jnp.concatenate([wetness[:, 1:], east_pair[1]], axis=1)
    wet_north = jnp.concatenate([wetness[1:, :], north_pair[1]], axis=0)
    mask_x = wetness * wet_east
    mask_y = wetness * wet_north
    depth_x = face_depth[0] * mask_x
    depth_y = face_depth[1] * mask_y
    flux_x = discharge[0] * mask_x
    flux_y = discharge[1] * mask_y
    for turn in range(OSTEPS):
        if turn == 0:
            east_col = east_pair[0]
            north_row = north_pair[0]
        else:
            east_col = passed_along(level[:, :1], "map", -1)
            north_row = passed_along(level[:1, :], "depth", -1)
        level_east = jnp.concatenate([level[:, 1:], east_col], axis=1)
        level_north = jnp.concatenate([level[1:, :], north_row], axis=0)
        flux_x = flux_x - ocean_step * gravity * depth_x * (level_east - level)
        flux_y = flux_y - ocean_step * gravity * depth_y * (level_north - level)
        west_col = passed_along(flux_x[:, -1:], "map", 1)
        south_row = passed_along(flux_y[-1:, :], "depth", 1)
        flux_west = jnp.concatenate([west_col, flux_x[:, :-1]], axis=1)
        flux_south = jnp.concatenate([south_row, flux_y[:-1, :]], axis=0)
        level = (
            level
            - ocean_step * wetness * (flux_x - flux_west + (flux_y - flux_south))
            + ocean_step * source
        )
    return (speeds, forces, level, jnp.stack([flux_x, flux_y]))


def solution(mesh):
    return jax.shard_map(
        per_device,
        mesh=mesh,
        in_specs=(
            P(None, "depth", "map", None),
            P(None, "depth", "map", None),
            P("depth", "map", None),
            P(),
            P(),
            P(),
            P("depth", "map"),
            P(None, "depth", "map"),
            P(None, "depth", "map"),
            P("depth", "map"),
            P("depth", "map"),
        ),
        out_specs=(
            P(None, "depth", "map", None),
            P(None, "depth", "map", None),
            P("depth", "map"),
            P(None, "depth", "map"),
        ),
        check_vma=False,
    )
```

profile of v0, /device:TPU:7, one launch (start us, length us, event | category | flops | bytes accessed | tf_op | source)
XLA Modules:
  0.0 251.1 jit_solution(1492550919271240779)
XLA Ops:
  2.3 3.7 %collective-permute-start = (f32[3,16,2,128]{3,2,1,0:T(2,128)}, f32[3,16,2,128]{3,2,1,0:T(2,128)}, u32[]{:S(2)}, u32[]{:S(2)}) collective-permute-start(f32[3,16,2,128]{3,2,1,0:T(2,128)} %get-tuple-element.138), channel_id=1, source_target_pairs={{0,1},{1,2},{2,3},{3,4},{4,5},{5,6},{6,7},{7,8},{8,9},{9,10},{10,1... | collective-permute-start | bytes 147464 | tf_op jit(solution)/shard_map/ppermute | solution.py:23
  6.0 1.9 collective-permute-start.1
  10.9 4.8 %collective-permute-start.3 = (f32[3,2,32,128]{3,2,1,0:T(8,128)}, f32[3,2,32,128]{3,2,1,0:T(8,128)}, u32[]{:S(2)}, u32[]{:S(2)}) collective-permute-start(f32[3,2,32,128]{3,2,1,0:T(8,128)} %get-tuple-element.143), channel_id=1, source_target_pairs={{16,0},{17,1},{18,2},{19,3},{20,4},{21,5},{22,6},{23,7},{24,8},{25... | collective-permute-start | bytes 294920 | tf_op jit(solution)/shard_map/ppermute | solution.py:24
  30.2 6.6 %fusion.30 = (f32[16,32,128]{2,1,0:T(8,128)S(1)}, f32[16,32,128]{2,1,0:T(8,128)S(1)}, pred[16,32,128]{2,1,0:T(8,128)(4,1)S(1)}, pred[16,32,128]{2,1,0:T(8,128)(4...) fusion(f32[3,16,32,128]{3,2,1,0:T(8,128)S(1)} %copy-done.1, ...), kind=kLoop, calls=%fused_computation.102 | loop fusion | flops 3211264 | bytes 4915232 | tf_op jit(solution)/shard_map/add | solution.py:125
  42.1 4.0 %collective-permute-start.5 = (f32[3,2,32,128]{3,2,1,0:T(8,128)S(1)}, f32[3,2,32,128]{3,2,1,0:T(8,128)S(1)}, u32[]{:S(2)}, u32[]{:S(2)}) collective-permute-start(f32[3,2,32,128]{3,2,1,0:T(8,128)S(1)} %get-tuple-element.190), channel_id=1, source_target_pairs={{16,0},{17,1},{18,2},{19,3},{20,4},{21,5},{22,6},{23,7},{24,8},{25... | collective-permute-start | bytes 294920 | tf_op jit(solution)/shard_map/ppermute | solution.py:24
  47.8 6.2 %collective-permute-start.6 = (f32[3,20,2,128]{3,2,1,0:T(2,128)S(1)}, f32[3,20,2,128]{3,2,1,0:T(2,128)S(1)}, u32[]{:S(2)}, u32[]{:S(2)}) collective-permute-start(f32[3,20,2,128]{3,2,1,0:T(2,128)S(1)} %get-tuple-element.160), channel_id=1, source_target_pairs={{0,1},{1,2},{2,3},{3,4},{4,5},{5,6},{6,7},{7,8},{8,9},{9,10},{10,1... | collective-permute-start | bytes 184328 | tf_op jit(solution)/shard_map/ppermute | solution.py:23
  54.0 1.9 collective-permute-start.7
  56.2 4.2 %collective-permute-done.7 = f32[3,20,2,128]{3,2,1,0:T(2,128)S(1)} collective-permute-done((f32[3,20,2,128]{3,2,1,0:T(2,128)S(1)}, f32[3,20,2,128]{3,2,1,0:T(2,128)S(1)}, u32[]{:S(2)}, u32[]{:S(2)}) %collective-permute-start.7) | collective-permute-done | bytes 61472 | tf_op jit(solution)/shard_map/ppermute | solution.py:24
  60.5 10.9 %multiply_add_fusion.3 = (f32[16,32,128]{2,1,0:T(8,128)S(1)}, f32[16,32,128]{2,1,0:T(8,128)S(1)}, f32[16,32,128]{2,1,0:T(8,128)S(1)}, f32[16,32,128]{2,1,0:T(8,1...) fusion(f32[6,16,32,128]{3,2,1,0:T(8,128)S(1)} %copy-done, ...), kind=kLoop, calls=%fused_computation.482 | loop fusion | flops 3670016 | bytes 5505088 | tf_op jit(solution)/shard_map/add | solution.py:155
  73.5 1.9 collective-permute-start.8
  75.4 2.4 collective-permute-start.9
  79.5 4.0 %collective-permute-start.11 = (f32[3,2,32,128]{3,2,1,0:T(8,128)S(1)}, f32[3,2,32,128]{3,2,1,0:T(8,128)S(1)}, u32[]{:S(2)}, u32[]{:S(2)}) collective-permute-start(f32[3,2,32,128]{3,2,1,0:T(8,128)S(1)} %get-tuple-element.185), channel_id=1, source_target_pairs={{16,0},{17,1},{18,2},{19,3},{20,4},{21,5},{22,6},{23,7},{24,8},{25... | collective-permute-start | bytes 294920 | tf_op jit(solution)/shard_map/ppermute | solution.py:24
  88.9 4.1 %collective-permute-start.13 = (f32[3,2,32,128]{3,2,1,0:T(8,128)S(1)}, f32[3,2,32,128]{3,2,1,0:T(8,128)S(1)}, u32[]{:S(2)}, u32[]{:S(2)}) collective-permute-start(f32[3,2,32,128]{3,2,1,0:T(8,128)S(1)} %get-tuple-element.180), channel_id=1, source_target_pairs={{16,0},{17,1},{18,2},{19,3},{20,4},{21,5},{22,6},{23,7},{24,8},{25... | collective-permute-start | bytes 294920 | tf_op jit(solution)/shard_map/ppermute | solution.py:24
  94.7 5.9 %collective-permute-start.14 = (f32[3,20,2,128]{3,2,1,0:T(2,128)S(1)}, f32[3,20,2,128]{3,2,1,0:T(2,128)S(1)}, u32[]{:S(2)}, u32[]{:S(2)}) collective-permute-start(f32[3,20,2,128]{3,2,1,0:T(2,128)S(1)} %get-tuple-element.155), channel_id=1, source_target_pairs={{0,1},{1,2},{2,3},{3,4},{4,5},{5,6},{6,7},{7,8},{8,9},{9,10},{10,1... | collective-permute-start | bytes 184328 | tf_op jit(solution)/shard_map/ppermute | solution.py:23
  100.6 2.1 collective-permute-start.15
  104.0 3.1 %collective-permute-done.15 = f32[3,20,2,128]{3,2,1,0:T(2,128)S(1)} collective-permute-done((f32[3,20,2,128]{3,2,1,0:T(2,128)S(1)}, f32[3,20,2,128]{3,2,1,0:T(2,128)S(1)}, u32[]{:S(2)}, u32[]{:S(2)}) %collective-permute-start.15) | collective-permute-done | bytes 61472 | tf_op jit(solution)/shard_map/ppermute | solution.py:24
  112.0 1.9 collective-permute-start.16
  113.9 2.4 collective-permute-start.17
  119.3 4.0 %collective-permute-start.19 = (f32[3,2,32,128]{3,2,1,0:T(8,128)S(1)}, f32[3,2,32,128]{3,2,1,0:T(8,128)S(1)}, u32[]{:S(2)}, u32[]{:S(2)}) collective-permute-start(f32[3,2,32,128]{3,2,1,0:T(8,128)S(1)} %get-tuple-element.175), channel_id=1, source_target_pairs={{16,0},{17,1},{18,2},{19,3},{20,4},{21,5},{22,6},{23,7},{24,8},{25... | collective-permute-start | bytes 294920 | tf_op jit(solution)/shard_map/ppermute | solution.py:24
  126.7 7.3 %psum.7 = f32[32,256]{1,0:T(8,128)S(1)} all-reduce(f32[32,256]{1,0:T(8,128)S(1)} %copy_bitcast_fusion), channel_id=1, replica_groups=mesh['depth'=2,'map'=16] {'depth'}, use_global_device_ids=true, to_apply=%region_0.1 | all-reduce | flops 8192 | bytes 65536 | tf_op jit(solution)/shard_map/psum | solution.py:31
  134.0 52.3 %while.13 = (s32[]{:T(128)}, f32[16,2,8,256]{3,2,1,0:T(8,128)}, s32[16,8,256]{2,1,0:T(8,128)}, f32[32,256]{1,0:T(8,128)S(1)}, s32[]{:T(128)}) while((s32[]{:T(128)}, f32[16,2,8,256]{3,2,1,0:T(8,128)}, s32[16,8,256]{2,1,0:T(8,128)}, f32[32,256]{1,0:T(8,128)S(1)}, s32[]{:T(128)}) %tuple.162), condition=%wide.region_4.5_spmd.clone, body=%wide.region_1.4_spmd.clone.sunk | while | flops 202754048 | bytes 4330053 | solution.py:98
  187.4 2.4 fusion.105
  196.6 5.0 %collective-permute-start.24 = (f32[2,128,1]{1,2,0:T(1,128)S(1)}, f32[2,128,1]{1,2,0:T(1,128)S(1)}, u32[]{:S(2)}, u32[]{:S(2)}) collective-permute-start(f32[2,128,1]{1,2,0:T(1,128)S(1)} %pad_maximum_fusion.64), channel_id=1, source_target_pairs={{1,0},{2,1},{3,2},{4,3},{5,4},{6,5},{7,6},{8,7},{9,8},{10,9},{11,1... | collective-permute-start | bytes 3080 | tf_op jit(solution)/shard_map/ppermute | solution.py:37
  206.8 4.6 %collective-permute-start.25 = (f32[128,1]{1,0:T(8,128)S(1)}, f32[128,1]{1,0:T(8,128)S(1)}, u32[]{:S(2)}, u32[]{:S(2)}) collective-permute-start(f32[128,1]{1,0:T(8,128)S(1)} %slice.2012), channel_id=1, source_target_pairs={{0,1},{1,2},{2,3},{3,4},{4,5},{5,6},{6,7},{7,8},{8,9},{9,10},{10,1... | collective-permute-start | bytes 1544 | tf_op jit(solution)/shard_map/ppermute | solution.py:37
  212.8 2.9 %collective-permute-done.27 = f32[1,256]{1,0:T(1,128)S(1)} collective-permute-done((f32[1,256]{1,0:T(1,128)S(1)}, f32[1,256]{1,0:T(1,128)S(1)}, u32[]{:S(2)}, u32[]{:S(2)}) %collective-permute-start.27) | collective-permute-done | bytes 1056 | tf_op jit(solution)/shard_map/ppermute | solution.py:37
  215.9 2.1 collective-permute-start.28
  221.4 4.0 %collective-permute-start.21 = (f32[3,2,32,128]{3,2,1,0:T(8,128)S(1)}, f32[3,2,32,128]{3,2,1,0:T(8,128)S(1)}, u32[]{:S(2)}, u32[]{:S(2)}) collective-permute-start(f32[3,2,32,128]{3,2,1,0:T(8,128)S(1)} %get-tuple-element.170), channel_id=1, source_target_pairs={{16,0},{17,1},{18,2},{19,3},{20,4},{21,5},{22,6},{23,7},{24,8},{25... | collective-permute-start | bytes 294920 | tf_op jit(solution)/shard_map/ppermute | solution.py:24
  225.8 5.4 %collective-permute-start.29 = (f32[128,1]{1,0:T(8,128)S(1)}, f32[128,1]{1,0:T(8,128)S(1)}, u32[]{:S(2)}, u32[]{:S(2)}) collective-permute-start(f32[128,1]{1,0:T(8,128)S(1)} %slice.2025), channel_id=1, source_target_pairs={{0,1},{1,2},{2,3},{3,4},{4,5},{5,6},{6,7},{7,8},{8,9},{9,10},{10,1... | collective-permute-start | bytes 1544 | tf_op jit(solution)/shard_map/ppermute | solution.py:37
  233.2 2.3 collective-permute-done.31
  236.3 3.1 %collective-permute-start.22 = (f32[3,20,2,128]{3,2,1,0:T(2,128)S(1)}, f32[3,20,2,128]{3,2,1,0:T(2,128)S(1)}, u32[]{:S(2)}, u32[]{:S(2)}) collective-permute-start(f32[3,20,2,128]{3,2,1,0:T(2,128)S(1)} %get-tuple-element.150), channel_id=1, source_target_pairs={{0,1},{1,2},{2,3},{3,4},{4,5},{5,6},{6,7},{7,8},{8,9},{9,10},{10,1... | collective-permute-start | bytes 184328 | tf_op jit(solution)/shard_map/ppermute | solution.py:23
  239.5 2.1 collective-permute-start.23
  241.8 4.2 %collective-permute-done.23 = f32[3,20,2,128]{3,2,1,0:T(2,128)S(1)} collective-permute-done((f32[3,20,2,128]{3,2,1,0:T(2,128)S(1)}, f32[3,20,2,128]{3,2,1,0:T(2,128)S(1)}, u32[]{:S(2)}, u32[]{:S(2)}) %collective-permute-start.23) | collective-permute-done | bytes 61472 | tf_op jit(solution)/shard_map/ppermute | solution.py:24
  (384 shorter events, 127.0 us)
Async XLA Ops:
  2.3 25.8 %collective-permute-start = (f32[3,16,2,128]{3,2,1,0:T(2,128)}, f32[3,16,2,128]{3,2,1,0:T(2,128)}, u32[]{:S(2)}, u32[]{:S(2)}) collective-permute-start(f32[3,16,2,128]{3,2,1,0:T(2,128)} %get-tuple-element.138), channel_id=1, source_target_pairs={{0,1},{1,2},{2,3},{3,4},{4,5},{5,6},{6,7},{7,8},{8,9},{9,10},{10,1... | collective-permute-start | bytes 147464 | tf_op jit(solution)/shard_map/ppermute | solution.py:23
  6.0 22.1 %collective-permute-start.1 = (f32[3,16,2,128]{3,2,1,0:T(2,128)}, f32[3,16,2,128]{3,2,1,0:T(2,128)}, u32[]{:S(2)}, u32[]{:S(2)}) collective-permute-start(f32[3,16,2,128]{3,2,1,0:T(2,128)} %get-tuple-element.139), channel_id=1, source_target_pairs={{1,0},{2,1},{3,2},{4,3},{5,4},{6,5},{7,6},{8,7},{9,8},{10,9},{11,1... | collective-permute-start | bytes 147464 | tf_op jit(solution)/shard_map/ppermute | solution.py:24
  9.6 19.8 %collective-permute-start.2 = (f32[3,2,32,128]{3,2,1,0:T(8,128)}, f32[3,2,32,128]{3,2,1,0:T(8,128)S(1)}, u32[]{:S(2)}, u32[]{:S(2)}) collective-permute-start(f32[3,2,32,128]{3,2,1,0:T(8,128)} %get-tuple-element.142), channel_id=1, source_target_pairs={{0,16},{1,17},{2,18},{3,19},{4,20},{5,21},{6,22},{7,23},{8,24},{9,... | collective-permute-start | bytes 294920 | tf_op jit(solution)/shard_map/ppermute | solution.py:23
  10.9 18.5 %collective-permute-start.3 = (f32[3,2,32,128]{3,2,1,0:T(8,128)}, f32[3,2,32,128]{3,2,1,0:T(8,128)}, u32[]{:S(2)}, u32[]{:S(2)}) collective-permute-start(f32[3,2,32,128]{3,2,1,0:T(8,128)} %get-tuple-element.143), channel_id=1, source_target_pairs={{16,0},{17,1},{18,2},{19,3},{20,4},{21,5},{22,6},{23,7},{24,8},{25... | collective-permute-start | bytes 294920 | tf_op jit(solution)/shard_map/ppermute | solution.py:24
  40.8 5.9 %collective-permute-start.4 = (f32[3,2,32,128]{3,2,1,0:T(8,128)S(1)}, f32[3,2,32,128]{3,2,1,0:T(8,128)S(1)}, u32[]{:S(2)}, u32[]{:S(2)}) collective-permute-start(f32[3,2,32,128]{3,2,1,0:T(8,128)S(1)} %get-tuple-element.189), channel_id=1, source_target_pairs={{0,16},{1,17},{2,18},{3,19},{4,20},{5,21},{6,22},{7,23},{8,24},{9,... | collective-permute-start | bytes 294920 | tf_op jit(solution)/shard_map/ppermute | solution.py:23
  42.1 5.6 %collective-permute-start.5 = (f32[3,2,32,128]{3,2,1,0:T(8,128)S(1)}, f32[3,2,32,128]{3,2,1,0:T(8,128)S(1)}, u32[]{:S(2)}, u32[]{:S(2)}) collective-permute-start(f32[3,2,32,128]{3,2,1,0:T(8,128)S(1)} %get-tuple-element.190), channel_id=1, source_target_pairs={{16,0},{17,1},{18,2},{19,3},{20,4},{21,5},{22,6},{23,7},{24,8},{25... | collective-permute-start | bytes 294920 | tf_op jit(solution)/shard_map/ppermute | solution.py:24
  47.8 8.4 %collective-permute-start.6 = (f32[3,20,2,128]{3,2,1,0:T(2,128)S(1)}, f32[3,20,2,128]{3,2,1,0:T(2,128)S(1)}, u32[]{:S(2)}, u32[]{:S(2)}) collective-permute-start(f32[3,20,2,128]{3,2,1,0:T(2,128)S(1)} %get-tuple-element.160), channel_id=1, source_target_pairs={{0,1},{1,2},{2,3},{3,4},{4,5},{5,6},{6,7},{7,8},{8,9},{9,10},{10,1... | collective-permute-start | bytes 184328 | tf_op jit(solution)/shard_map/ppermute | solution.py:23
  54.0 6.4 %collective-permute-start.7 = (f32[3,20,2,128]{3,2,1,0:T(2,128)S(1)}, f32[3,20,2,128]{3,2,1,0:T(2,128)S(1)}, u32[]{:S(2)}, u32[]{:S(2)}) collective-permute-start(f32[3,20,2,128]{3,2,1,0:T(2,128)S(1)} %get-tuple-element.161), channel_id=1, source_target_pairs={{1,0},{2,1},{3,2},{4,3},{5,4},{6,5},{7,6},{8,7},{9,8},{10,9},{11,1... | collective-permute-start | bytes 184328 | tf_op jit(solution)/shard_map/ppermute | solution.py:24
  73.5 10.1 %collective-permute-start.8 = (f32[3,16,2,128]{3,2,1,0:T(2,128)S(1)}, f32[3,16,2,128]{3,2,1,0:T(2,128)S(1)}, u32[]{:S(2)}, u32[]{:S(2)}) collective-permute-start(f32[3,16,2,128]{3,2,1,0:T(2,128)S(1)} %get-tuple-element.181), channel_id=1, source_target_pairs={{0,1},{1,2},{2,3},{3,4},{4,5},{5,6},{6,7},{7,8},{8,9},{9,10},{10,1... | collective-permute-start | bytes 147464 | tf_op jit(solution)/shard_map/ppermute | solution.py:23
  75.4 8.2 %collective-permute-start.9 = (f32[3,16,2,128]{3,2,1,0:T(2,128)S(1)}, f32[3,16,2,128]{3,2,1,0:T(2,128)S(1)}, u32[]{:S(2)}, u32[]{:S(2)}) collective-permute-start(f32[3,16,2,128]{3,2,1,0:T(2,128)S(1)} %get-tuple-element.182), channel_id=1, source_target_pairs={{1,0},{2,1},{3,2},{4,3},{5,4},{6,5},{7,6},{8,7},{9,8},{10,9},{11,1... | collective-permute-start | bytes 147464 | tf_op jit(solution)/shard_map/ppermute | solution.py:24
  78.2 6.3 %collective-permute-start.10 = (f32[3,2,32,128]{3,2,1,0:T(8,128)S(1)}, f32[3,2,32,128]{3,2,1,0:T(8,128)S(1)}, u32[]{:S(2)}, u32[]{:S(2)}) collective-permute-start(f32[3,2,32,128]{3,2,1,0:T(8,128)S(1)} %get-tuple-element.186), channel_id=1, source_target_pairs={{0,16},{1,17},{2,18},{3,19},{4,20},{5,21},{6,22},{7,23},{8,24},{9,... | collective-permute-start | bytes 294920 | tf_op jit(solution)/shard_map/ppermute | solution.py:23
  79.5 5.9 %collective-permute-start.11 = (f32[3,2,32,128]{3,2,1,0:T(8,128)S(1)}, f32[3,2,32,128]{3,2,1,0:T(8,128)S(1)}, u32[]{:S(2)}, u32[]{:S(2)}) collective-permute-start(f32[3,2,32,128]{3,2,1,0:T(8,128)S(1)} %get-tuple-element.185), channel_id=1, source_target_pairs={{16,0},{17,1},{18,2},{19,3},{20,4},{21,5},{22,6},{23,7},{24,8},{25... | collective-permute-start | bytes 294920 | tf_op jit(solution)/shard_map/ppermute | solution.py:24
  87.6 6.0 %collective-permute-start.12 = (f32[3,2,32,128]{3,2,1,0:T(8,128)S(1)}, f32[3,2,32,128]{3,2,1,0:T(8,128)S(1)}, u32[]{:S(2)}, u32[]{:S(2)}) collective-permute-start(f32[3,2,32,128]{3,2,1,0:T(8,128)S(1)} %get-tuple-element.179), channel_id=1, source_target_pairs={{0,16},{1,17},{2,18},{3,19},{4,20},{5,21},{6,22},{7,23},{8,24},{9,... | collective-permute-start | bytes 294920 | tf_op jit(solution)/shard_map/ppermute | solution.py:23
  88.9 5.7 %collective-permute-start.13 = (f32[3,2,32,128]{3,2,1,0:T(8,128)S(1)}, f32[3,2,32,128]{3,2,1,0:T(8,128)S(1)}, u32[]{:S(2)}, u32[]{:S(2)}) collective-permute-start(f32[3,2,32,128]{3,2,1,0:T(8,128)S(1)} %get-tuple-element.180), channel_id=1, source_target_pairs={{16,0},{17,1},{18,2},{19,3},{20,4},{21,5},{22,6},{23,7},{24,8},{25... | collective-permute-start | bytes 294920 | tf_op jit(solution)/shard_map/ppermute | solution.py:24
  94.7 9.3 %collective-permute-start.14 = (f32[3,20,2,128]{3,2,1,0:T(2,128)S(1)}, f32[3,20,2,128]{3,2,1,0:T(2,128)S(1)}, u32[]{:S(2)}, u32[]{:S(2)}) collective-permute-start(f32[3,20,2,128]{3,2,1,0:T(2,128)S(1)} %get-tuple-element.155), channel_id=1, source_target_pairs={{0,1},{1,2},{2,3},{3,4},{4,5},{5,6},{6,7},{7,8},{8,9},{9,10},{10,1... | collective-permute-start | bytes 184328 | tf_op jit(solution)/shard_map/ppermute | solution.py:23
  100.6 6.4 %collective-permute-start.15 = (f32[3,20,2,128]{3,2,1,0:T(2,128)S(1)}, f32[3,20,2,128]{3,2,1,0:T(2,128)S(1)}, u32[]{:S(2)}, u32[]{:S(2)}) collective-permute-start(f32[3,20,2,128]{3,2,1,0:T(2,128)S(1)} %get-tuple-element.156), channel_id=1, source_target_pairs={{1,0},{2,1},{3,2},{4,3},{5,4},{6,5},{7,6},{8,7},{9,8},{10,9},{11,1... | collective-permute-start | bytes 184328 | tf_op jit(solution)/shard_map/ppermute | solution.py:24
  112.0 11.4 %collective-permute-start.16 = (f32[3,16,2,128]{3,2,1,0:T(2,128)S(1)}, f32[3,16,2,128]{3,2,1,0:T(2,128)S(1)}, u32[]{:S(2)}, u32[]{:S(2)}) collective-permute-start(f32[3,16,2,128]{3,2,1,0:T(2,128)S(1)} %get-tuple-element.171), channel_id=1, source_target_pairs={{0,1},{1,2},{2,3},{3,4},{4,5},{5,6},{6,7},{7,8},{8,9},{9,10},{10,1... | collective-permute-start | bytes 147464 | tf_op jit(solution)/shard_map/ppermute | solution.py:23
  113.9 9.5 %collective-permute-start.17 = (f32[3,16,2,128]{3,2,1,0:T(2,128)S(1)}, f32[3,16,2,128]{3,2,1,0:T(2,128)S(1)}, u32[]{:S(2)}, u32[]{:S(2)}) collective-permute-start(f32[3,16,2,128]{3,2,1,0:T(2,128)S(1)} %get-tuple-element.172), channel_id=1, source_target_pairs={{1,0},{2,1},{3,2},{4,3},{5,4},{6,5},{7,6},{8,7},{9,8},{10,9},{11,1... | collective-permute-start | bytes 147464 | tf_op jit(solution)/shard_map/ppermute | solution.py:24
  118.1 6.4 %collective-permute-start.18 = (f32[3,2,32,128]{3,2,1,0:T(8,128)S(1)}, f32[3,2,32,128]{3,2,1,0:T(8,128)S(1)}, u32[]{:S(2)}, u32[]{:S(2)}) collective-permute-start(f32[3,2,32,128]{3,2,1,0:T(8,128)S(1)} %get-tuple-element.176), channel_id=1, source_target_pairs={{0,16},{1,17},{2,18},{3,19},{4,20},{5,21},{6,22},{7,23},{8,24},{9,... | collective-permute-start | bytes 294920 | tf_op jit(solution)/shard_map/ppermute | solution.py:23
  119.3 5.9 %collective-permute-start.19 = (f32[3,2,32,128]{3,2,1,0:T(8,128)S(1)}, f32[3,2,32,128]{3,2,1,0:T(8,128)S(1)}, u32[]{:S(2)}, u32[]{:S(2)}) collective-permute-start(f32[3,2,32,128]{3,2,1,0:T(8,128)S(1)} %get-tuple-element.175), channel_id=1, source_target_pairs={{16,0},{17,1},{18,2},{19,3},{20,4},{21,5},{22,6},{23,7},{24,8},{25... | collective-permute-start | bytes 294920 | tf_op jit(solution)/shard_map/ppermute | solution.py:24
  196.6 8.2 %collective-permute-start.24 = (f32[2,128,1]{1,2,0:T(1,128)S(1)}, f32[2,128,1]{1,2,0:T(1,128)S(1)}, u32[]{:S(2)}, u32[]{:S(2)}) collective-permute-start(f32[2,128,1]{1,2,0:T(1,128)S(1)} %pad_maximum_fusion.64), channel_id=1, source_target_pairs={{1,0},{2,1},{3,2},{4,3},{5,4},{6,5},{7,6},{8,7},{9,8},{10,9},{11,1... | collective-permute-start | bytes 3080 | tf_op jit(solution)/shard_map/ppermute | solution.py:37
  203.1 2.4 collective-permute-start.26
  206.8 6.0 %collective-permute-start.25 = (f32[128,1]{1,0:T(8,128)S(1)}, f32[128,1]{1,0:T(8,128)S(1)}, u32[]{:S(2)}, u32[]{:S(2)}) collective-permute-start(f32[128,1]{1,0:T(8,128)S(1)} %slice.2012), channel_id=1, source_target_pairs={{0,1},{1,2},{2,3},{3,4},{4,5},{5,6},{6,7},{7,8},{8,9},{9,10},{10,1... | collective-permute-start | bytes 1544 | tf_op jit(solution)/shard_map/ppermute | solution.py:37
  211.4 4.3 %collective-permute-start.27 = (f32[1,256]{1,0:T(1,128)S(1)}, f32[1,256]{1,0:T(1,128)S(1)}, u32[]{:S(2)}, u32[]{:S(2)}) collective-permute-start(f32[1,256]{1,0:T(1,128)S(1)} %slice.2020), channel_id=1, source_target_pairs={{0,16},{1,17},{2,18},{3,19},{4,20},{5,21},{6,22},{7,23},{8,24},{9,... | collective-permute-start | bytes 3080 | tf_op jit(solution)/shard_map/ppermute | solution.py:37
  215.9 9.6 %collective-permute-start.28 = (f32[128,1]{1,0:T(8,128)S(1)}, f32[128,1]{1,0:T(8,128)S(1)}, u32[]{:S(2)}, u32[]{:S(2)}) collective-permute-start(f32[128,1]{1,0:T(8,128)S(1)} %slice.2024), channel_id=1, source_target_pairs={{1,0},{2,1},{3,2},{4,3},{5,4},{6,5},{7,6},{8,7},{9,8},{10,9},{11,1... | collective-permute-start | bytes 1544 | tf_op jit(solution)/shard_map/ppermute | solution.py:37
  218.0 7.6 %collective-permute-start.30 = (f32[1,256]{1,0:T(1,128)S(1)}, f32[1,256]{1,0:T(1,128)S(1)}, u32[]{:S(2)}, u32[]{:S(2)}) collective-permute-start(f32[1,256]{1,0:T(1,128)S(1)} %slice.2028), channel_id=1, source_target_pairs={{16,0},{17,1},{18,2},{19,3},{20,4},{21,5},{22,6},{23,7},{24,8},{25... | collective-permute-start | bytes 3080 | tf_op jit(solution)/shard_map/ppermute | solution.py:37
  220.1 16.2 %collective-permute-start.20 = (f32[3,2,32,128]{3,2,1,0:T(8,128)S(1)}, f32[3,2,32,128]{3,2,1,0:T(8,128)S(1)}, u32[]{:S(2)}, u32[]{:S(2)}) collective-permute-start(f32[3,2,32,128]{3,2,1,0:T(8,128)S(1)} %get-tuple-element.169), channel_id=1, source_target_pairs={{0,16},{1,17},{2,18},{3,19},{4,20},{5,21},{6,22},{7,23},{8,24},{9,... | collective-permute-start | bytes 294920 | tf_op jit(solution)/shard_map/ppermute | solution.py:23
  221.4 14.9 %collective-permute-start.21 = (f32[3,2,32,128]{3,2,1,0:T(8,128)S(1)}, f32[3,2,32,128]{3,2,1,0:T(8,128)S(1)}, u32[]{:S(2)}, u32[]{:S(2)}) collective-permute-start(f32[3,2,32,128]{3,2,1,0:T(8,128)S(1)} %get-tuple-element.170), channel_id=1, source_target_pairs={{16,0},{17,1},{18,2},{19,3},{20,4},{21,5},{22,6},{23,7},{24,8},{25... | collective-permute-start | bytes 294920 | tf_op jit(solution)/shard_map/ppermute | solution.py:24
  225.8 7.4 %collective-permute-start.29 = (f32[128,1]{1,0:T(8,128)S(1)}, f32[128,1]{1,0:T(8,128)S(1)}, u32[]{:S(2)}, u32[]{:S(2)}) collective-permute-start(f32[128,1]{1,0:T(8,128)S(1)} %slice.2025), channel_id=1, source_target_pairs={{0,1},{1,2},{2,3},{3,4},{4,5},{5,6},{6,7},{7,8},{8,9},{9,10},{10,1... | collective-permute-start | bytes 1544 | tf_op jit(solution)/shard_map/ppermute | solution.py:37
  231.2 4.3 %collective-permute-start.31 = (f32[1,256]{1,0:T(1,128)S(1)}, f32[1,256]{1,0:T(1,128)S(1)}, u32[]{:S(2)}, u32[]{:S(2)}) collective-permute-start(f32[1,256]{1,0:T(1,128)S(1)} %slice.2029), channel_id=1, source_target_pairs={{0,16},{1,17},{2,18},{3,19},{4,20},{5,21},{6,22},{7,23},{8,24},{9,... | collective-permute-start | bytes 3080 | tf_op jit(solution)/shard_map/ppermute | solution.py:37
  236.3 5.5 %collective-permute-start.22 = (f32[3,20,2,128]{3,2,1,0:T(2,128)S(1)}, f32[3,20,2,128]{3,2,1,0:T(2,128)S(1)}, u32[]{:S(2)}, u32[]{:S(2)}) collective-permute-start(f32[3,20,2,128]{3,2,1,0:T(2,128)S(1)} %get-tuple-element.150), channel_id=1, source_target_pairs={{0,1},{1,2},{2,3},{3,4},{4,5},{5,6},{6,7},{7,8},{8,9},{9,10},{10,1... | collective-permute-start | bytes 184328 | tf_op jit(solution)/shard_map/ppermute | solution.py:23
  239.5 6.6 %collective-permute-start.23 = (f32[3,20,2,128]{3,2,1,0:T(2,128)S(1)}, f32[3,20,2,128]{3,2,1,0:T(2,128)S(1)}, u32[]{:S(2)}, u32[]{:S(2)}) collective-permute-start(f32[3,20,2,128]{3,2,1,0:T(2,128)S(1)} %get-tuple-element.151), channel_id=1, source_target_pairs={{1,0},{2,1},{3,2},{4,3},{5,4},{6,5},{7,6},{8,7},{9,8},{10,9},{11,1... | collective-permute-start | bytes 184328 | tf_op jit(solution)/shard_map/ppermute | solution.py:24
  (64 other events, 339.4 us)
where the time goes:
time: 254 us; the launch traced here: 251 us
  starting transfers between devices  91.2 us (36%)
  other arithmetic  72.3 us (28%)
  local copies, waits for them, and re-layouts  39.5 us (16%)
  waiting for transfers between devices  21.9 us (9%)
  matrix products  16.4 us (6%)
  blocking collectives  7.31 us (3%)
    ppermute x12, starting transfers between devices, extended(): after = lax.ppermute(leading, axis, down)  37.7 us
    ppermute x12, starting transfers between devices, extended(): before = lax.ppermute(last, axis, up)  30.5 us
    ppermute x8, starting transfers between devices, passed_along(): return lax.ppermute(x, axis, pairs)  23 us
    dot_general x16, matrix products, one_block(): jnp.einsum('rck,kn->rcn', onehot, table, precision=lax.Precision.HIGHEST)  16.4 us
    ppermute x12, waiting for transfers between devices, extended(): after = lax.ppermute(leading, axis, down)  15.4 us
    select_n x16, other arithmetic, one_block(): lower = indices % tile_cols  11.3 us
    select_n x16, other arithmetic, one_block(): upper = indices // tile_cols  11.3 us
    add x2, other arithmetic, per_device(): forces[5] + time_step * (lame * spread + 2.0 * shear * strain_y)  11.2 us
  transfers between devices with their start and end apart: 32, of which 11 were waited for; matrix products, arithmetic and copies ran while one was open for 10% of the time, Pallas kernels for 0%

commit v1 on v0

--- a/solution.py
+++ b/solution.py
@@ -28,7 +28,7 @@
 
 def broadcast(x, axis, root):
     mine = lax.axis_index(axis) == root
-    return lax.psum(jnp.where(mine, x, jnp.zeros_like(x)), axis)
+    return jnp.sum(lax.all_gather(jnp.where(mine, x, jnp.zeros_like(x)), axis), axis=0)
 
 
 def passed_along(x, axis, by):

time: 254 us -> 250 us (0.984)
  blocking collectives: 7.31 us -> 4.15 us
    psum x1 -> x0, blocking collectives: 7.31 us -> none  [broadcast(): return lax.psum(jnp.where(mine, x, jnp.zeros_like(x)), axis)]
    all_gather x0 -> x1, blocking collectives: none -> 4.15 us  [broadcast(): lax.all_gather(jnp.where(mine, x, jnp.zeros_like(x)), axis)]
    unnamed x128 -> x122, local copies, waits for them, and re-layouts: 5.89 us -> 5.83 us
where the time goes in v1:
time: 250 us; the launch traced here: 247 us
  starting transfers between devices  91.3 us (37%)
  other arithmetic  72.2 us (29%)
  local copies, waits for them, and re-layouts  38 us (15%)
  waiting for transfers between devices  22 us (9%)
  matrix products  16.4 us (7%)
  blocking collectives  4.15 us (2%)
    ppermute x12, starting transfers between devices, extended(): after = lax.ppermute(leading, axis, down)  37.1 us
    ppermute x12, starting transfers between devices, extended(): before = lax.ppermute(last, axis, up)  30.5 us
    ppermute x8, starting transfers between devices, passed_along(): return lax.ppermute(x, axis, pairs)  23.8 us
    dot_general x16, matrix products, one_block(): jnp.einsum('rck,kn->rcn', onehot, table, precision=lax.Precision.HIGHEST)  16.4 us
    ppermute x12, waiting for transfers between devices, extended(): after = lax.ppermute(leading, axis, down)  15.5 us
    select_n x16, other arithmetic, one_block(): lower = indices % tile_cols  11.3 us
    select_n x16, other arithmetic, one_block(): upper = indices // tile_cols  11.3 us
    add x2, other arithmetic, per_device(): forces[5] + time_step * (lame * spread + 2.0 * shear * strain_y)  11 us
  transfers between devices with their start and end apart: 32, of which 11 were waited for; matrix products, arithmetic and copies ran while one was open for 10% of the time, Pallas kernels for 0%

profile of v1, /device:TPU:7, one launch (start us, length us, event | category | flops | bytes accessed | tf_op | source)
XLA Modules:
  0.0 246.7 jit_solution(6693777967262925130)
XLA Ops:
  1.7 3.7 %collective-permute-start = (f32[3,16,2,128]{3,2,1,0:T(2,128)S(1)}, f32[3,16,2,128]{3,2,1,0:T(2,128)}, u32[]{:S(2)}, u32[]{:S(2)}) collective-permute-start(f32[3,16,2,128]{3,2,1,0:T(2,128)S(1)} %get-tuple-element.138), channel_id=1, source_target_pairs={{0,1},{1,2},{2,3},{3,4},{4,5},{5,6},{6,7},{7,8},{8,9},{9,10},{10,1... | collective-permute-start | bytes 147464 | tf_op jit(solution)/shard_map/ppermute | solution.py:23
  5.4 1.9 collective-permute-start.1
  10.2 4.1 %collective-permute-start.3 = (f32[3,2,32,128]{3,2,1,0:T(8,128)S(1)}, f32[3,2,32,128]{3,2,1,0:T(8,128)S(1)}, u32[]{:S(2)}, u32[]{:S(2)}) collective-permute-start(f32[3,2,32,128]{3,2,1,0:T(8,128)S(1)} %get-tuple-element.143), channel_id=1, source_target_pairs={{16,0},{17,1},{18,2},{19,3},{20,4},{21,5},{22,6},{23,7},{24,8},{25... | collective-permute-start | bytes 294920 | tf_op jit(solution)/shard_map/ppermute | solution.py:24
  29.1 6.5 %fusion.30 = (f32[16,32,128]{2,1,0:T(8,128)S(1)}, f32[16,32,128]{2,1,0:T(8,128)S(1)}, pred[16,32,128]{2,1,0:T(8,128)(4,1)S(1)}, pred[16,32,128]{2,1,0:T(8,128)(4...) fusion(f32[3,16,32,128]{3,2,1,0:T(8,128)S(1)} %copy-done.1, ...), kind=kLoop, calls=%fused_computation.102 | loop fusion | flops 3211264 | bytes 4915232 | tf_op jit(solution)/shard_map/add | solution.py:125
  39.3 4.0 %collective-permute-start.5 = (f32[3,2,32,128]{3,2,1,0:T(8,128)S(1)}, f32[3,2,32,128]{3,2,1,0:T(8,128)S(1)}, u32[]{:S(2)}, u32[]{:S(2)}) collective-permute-start(f32[3,2,32,128]{3,2,1,0:T(8,128)S(1)} %get-tuple-element.190), channel_id=1, source_target_pairs={{16,0},{17,1},{18,2},{19,3},{20,4},{21,5},{22,6},{23,7},{24,8},{25... | collective-permute-start | bytes 294920 | tf_op jit(solution)/shard_map/ppermute | solution.py:24
  45.0 6.2 %collective-permute-start.6 = (f32[3,20,2,128]{3,2,1,0:T(2,128)S(1)}, f32[3,20,2,128]{3,2,1,0:T(2,128)S(1)}, u32[]{:S(2)}, u32[]{:S(2)}) collective-permute-start(f32[3,20,2,128]{3,2,1,0:T(2,128)S(1)} %get-tuple-element.160), channel_id=1, source_target_pairs={{0,1},{1,2},{2,3},{3,4},{4,5},{5,6},{6,7},{7,8},{8,9},{9,10},{10,1... | collective-permute-start | bytes 184328 | tf_op jit(solution)/shard_map/ppermute | solution.py:23
  51.3 1.9 collective-permute-start.7
  53.4 4.2 %collective-permute-done.7 = f32[3,20,2,128]{3,2,1,0:T(2,128)S(1)} collective-permute-done((f32[3,20,2,128]{3,2,1,0:T(2,128)S(1)}, f32[3,20,2,128]{3,2,1,0:T(2,128)S(1)}, u32[]{:S(2)}, u32[]{:S(2)}) %collective-permute-start.7) | collective-permute-done | bytes 61472 | tf_op jit(solution)/shard_map/ppermute | solution.py:24
  57.8 10.7 %multiply_add_fusion.3 = (f32[16,32,128]{2,1,0:T(8,128)S(1)}, f32[16,32,128]{2,1,0:T(8,128)S(1)}, f32[16,32,128]{2,1,0:T(8,128)S(1)}, f32[16,32,128]{2,1,0:T(8,1...) fusion(f32[6,16,32,128]{3,2,1,0:T(8,128)S(1)} %copy-done, ...), kind=kLoop, calls=%fused_computation.482 | loop fusion | flops 3670016 | bytes 5505088 | tf_op jit(solution)/shard_map/add | solution.py:155
  70.5 1.9 collective-permute-start.8
  72.5 2.4 collective-permute-start.9
  76.6 4.0 %collective-permute-start.11 = (f32[3,2,32,128]{3,2,1,0:T(8,128)S(1)}, f32[3,2,32,128]{3,2,1,0:T(8,128)S(1)}, u32[]{:S(2)}, u32[]{:S(2)}) collective-permute-start(f32[3,2,32,128]{3,2,1,0:T(8,128)S(1)} %get-tuple-element.185), channel_id=1, source_target_pairs={{16,0},{17,1},{18,2},{19,3},{20,4},{21,5},{22,6},{23,7},{24,8},{25... | collective-permute-start | bytes 294920 | tf_op jit(solution)/shard_map/ppermute | solution.py:24
  86.0 4.1 %collective-permute-start.13 = (f32[3,2,32,128]{3,2,1,0:T(8,128)S(1)}, f32[3,2,32,128]{3,2,1,0:T(8,128)S(1)}, u32[]{:S(2)}, u32[]{:S(2)}) collective-permute-start(f32[3,2,32,128]{3,2,1,0:T(8,128)S(1)} %get-tuple-element.180), channel_id=1, source_target_pairs={{16,0},{17,1},{18,2},{19,3},{20,4},{21,5},{22,6},{23,7},{24,8},{25... | collective-permute-start | bytes 294920 | tf_op jit(solution)/shard_map/ppermute | solution.py:24
  91.8 5.9 %collective-permute-start.14 = (f32[3,20,2,128]{3,2,1,0:T(2,128)S(1)}, f32[3,20,2,128]{3,2,1,0:T(2,128)S(1)}, u32[]{:S(2)}, u32[]{:S(2)}) collective-permute-start(f32[3,20,2,128]{3,2,1,0:T(2,128)S(1)} %get-tuple-element.155), channel_id=1, source_target_pairs={{0,1},{1,2},{2,3},{3,4},{4,5},{5,6},{6,7},{7,8},{8,9},{9,10},{10,1... | collective-permute-start | bytes 184328 | tf_op jit(solution)/shard_map/ppermute | solution.py:23
  97.7 2.1 collective-permute-start.15
  101.0 3.1 %collective-permute-done.15 = f32[3,20,2,128]{3,2,1,0:T(2,128)S(1)} collective-permute-done((f32[3,20,2,128]{3,2,1,0:T(2,128)S(1)}, f32[3,20,2,128]{3,2,1,0:T(2,128)S(1)}, u32[]{:S(2)}, u32[]{:S(2)}) %collective-permute-start.15) | collective-permute-done | bytes 61472 | tf_op jit(solution)/shard_map/ppermute | solution.py:24
  111.0 2.4 collective-permute-start.17
  116.4 4.0 %collective-permute-start.19 = (f32[3,2,32,128]{3,2,1,0:T(8,128)S(1)}, f32[3,2,32,128]{3,2,1,0:T(8,128)S(1)}, u32[]{:S(2)}, u32[]{:S(2)}) collective-permute-start(f32[3,2,32,128]{3,2,1,0:T(8,128)S(1)} %get-tuple-element.175), channel_id=1, source_target_pairs={{16,0},{17,1},{18,2},{19,3},{20,4},{21,5},{22,6},{23,7},{24,8},{25... | collective-permute-start | bytes 294920 | tf_op jit(solution)/shard_map/ppermute | solution.py:24
  123.8 4.2 %all_gather.4 = f32[2,2,32,128]{3,2,1,0:T(8,128)S(1)} all-gather(f32[1,2,32,128]{3,2,1,0:T(8,128)S(1)} %maximum_select_fusion), channel_id=1, replica_groups=mesh['depth'=2,'map'=16] {'depth'}, dimensions={0}, use_global_device_ids=true | all-gather | bytes 98304 | tf_op jit(solution)/shard_map/all_gather | solution.py:31
  128.0 52.3 %while.13 = (s32[]{:T(128)}, f32[16,2,8,256]{3,2,1,0:T(8,128)}, s32[16,8,256]{2,1,0:T(8,128)}, f32[32,256]{1,0:T(8,128)S(1)}, s32[]{:T(128)}) while((s32[]{:T(128)}, f32[16,2,8,256]{3,2,1,0:T(8,128)}, s32[16,8,256]{2,1,0:T(8,128)}, f32[32,256]{1,0:T(8,128)S(1)}, s32[]{:T(128)}) %tuple.162), condition=%wide.region_4.5_spmd.clone, body=%wide.region_1.4_spmd.clone.sunk | while | flops 202754048 | bytes 4330053 | solution.py:98
  181.4 2.0 fusion.105
  190.1 3.9 %collective-permute-start.24 = (f32[2,128,1]{1,2,0:T(1,128)S(1)}, f32[2,128,1]{1,2,0:T(1,128)S(1)}, u32[]{:S(2)}, u32[]{:S(2)}) collective-permute-start(f32[2,128,1]{1,2,0:T(1,128)S(1)} %pad_maximum_fusion.64), channel_id=1, source_target_pairs={{1,0},{2,1},{3,2},{4,3},{5,4},{6,5},{7,6},{8,7},{9,8},{10,9},{11,1... | collective-permute-start | bytes 3080 | tf_op jit(solution)/shard_map/ppermute | solution.py:37
  194.8 3.6 %collective-permute-start.26 = (f32[2,1,256]{2,1,0:T(1,128)S(1)}, f32[2,1,256]{2,1,0:T(1,128)S(1)}, u32[]{:S(2)}, u32[]{:S(2)}) collective-permute-start(f32[2,1,256]{2,1,0:T(1,128)S(1)} %pad_maximum_fusion.63), channel_id=1, source_target_pairs={{16,0},{17,1},{18,2},{19,3},{20,4},{21,5},{22,6},{23,7},{24,8},{25... | collective-permute-start | bytes 6152 | tf_op jit(solution)/shard_map/ppermute | solution.py:37
  200.7 4.6 %collective-permute-start.25 = (f32[128,1]{1,0:T(8,128)S(1)}, f32[128,1]{1,0:T(8,128)S(1)}, u32[]{:S(2)}, u32[]{:S(2)}) collective-permute-start(f32[128,1]{1,0:T(8,128)S(1)} %slice.2012), channel_id=1, source_target_pairs={{0,1},{1,2},{2,3},{3,4},{4,5},{5,6},{6,7},{7,8},{8,9},{9,10},{10,1... | collective-permute-start | bytes 1544 | tf_op jit(solution)/shard_map/ppermute | solution.py:37
  206.6 2.9 %collective-permute-done.27 = f32[1,256]{1,0:T(1,128)S(1)} collective-permute-done((f32[1,256]{1,0:T(1,128)S(1)}, f32[1,256]{1,0:T(1,128)S(1)}, u32[]{:S(2)}, u32[]{:S(2)}) %collective-permute-start.27) | collective-permute-done | bytes 1056 | tf_op jit(solution)/shard_map/ppermute | solution.py:37
  210.6 2.1 collective-permute-start.28
  216.1 4.0 %collective-permute-start.21 = (f32[3,2,32,128]{3,2,1,0:T(8,128)S(1)}, f32[3,2,32,128]{3,2,1,0:T(8,128)S(1)}, u32[]{:S(2)}, u32[]{:S(2)}) collective-permute-start(f32[3,2,32,128]{3,2,1,0:T(8,128)S(1)} %get-tuple-element.170), channel_id=1, source_target_pairs={{16,0},{17,1},{18,2},{19,3},{20,4},{21,5},{22,6},{23,7},{24,8},{25... | collective-permute-start | bytes 294920 | tf_op jit(solution)/shard_map/ppermute | solution.py:24
  220.5 5.4 %collective-permute-start.29 = (f32[128,1]{1,0:T(8,128)S(1)}, f32[128,1]{1,0:T(8,128)S(1)}, u32[]{:S(2)}, u32[]{:S(2)}) collective-permute-start(f32[128,1]{1,0:T(8,128)S(1)} %slice.2025), channel_id=1, source_target_pairs={{0,1},{1,2},{2,3},{3,4},{4,5},{5,6},{6,7},{7,8},{8,9},{9,10},{10,1... | collective-permute-start | bytes 1544 | tf_op jit(solution)/shard_map/ppermute | solution.py:37
  227.9 2.3 collective-permute-done.31
  231.9 3.1 %collective-permute-start.22 = (f32[3,20,2,128]{3,2,1,0:T(2,128)S(1)}, f32[3,20,2,128]{3,2,1,0:T(2,128)S(1)}, u32[]{:S(2)}, u32[]{:S(2)}) collective-permute-start(f32[3,20,2,128]{3,2,1,0:T(2,128)S(1)} %get-tuple-element.150), channel_id=1, source_target_pairs={{0,1},{1,2},{2,3},{3,4},{4,5},{5,6},{6,7},{7,8},{8,9},{9,10},{10,1... | collective-permute-start | bytes 184328 | tf_op jit(solution)/shard_map/ppermute | solution.py:23
  235.0 2.1 collective-permute-start.23
  237.4 4.2 %collective-permute-done.23 = f32[3,20,2,128]{3,2,1,0:T(2,128)S(1)} collective-permute-done((f32[3,20,2,128]{3,2,1,0:T(2,128)S(1)}, f32[3,20,2,128]{3,2,1,0:T(2,128)S(1)}, u32[]{:S(2)}, u32[]{:S(2)}) %collective-permute-start.23) | collective-permute-done | bytes 61472 | tf_op jit(solution)/shard_map/ppermute | solution.py:24
  (380 shorter events, 126.5 us)
Async XLA Ops:
  1.7 25.1 %collective-permute-start = (f32[3,16,2,128]{3,2,1,0:T(2,128)S(1)}, f32[3,16,2,128]{3,2,1,0:T(2,128)}, u32[]{:S(2)}, u32[]{:S(2)}) collective-permute-start(f32[3,16,2,128]{3,2,1,0:T(2,128)S(1)} %get-tuple-element.138), channel_id=1, source_target_pairs={{0,1},{1,2},{2,3},{3,4},{4,5},{5,6},{6,7},{7,8},{8,9},{9,10},{10,1... | collective-permute-start | bytes 147464 | tf_op jit(solution)/shard_map/ppermute | solution.py:23
  5.4 21.4 %collective-permute-start.1 = (f32[3,16,2,128]{3,2,1,0:T(2,128)S(1)}, f32[3,16,2,128]{3,2,1,0:T(2,128)}, u32[]{:S(2)}, u32[]{:S(2)}) collective-permute-start(f32[3,16,2,128]{3,2,1,0:T(2,128)S(1)} %get-tuple-element.139), channel_id=1, source_target_pairs={{1,0},{2,1},{3,2},{4,3},{5,4},{6,5},{7,6},{8,7},{9,8},{10,9},{11,1... | collective-permute-start | bytes 147464 | tf_op jit(solution)/shard_map/ppermute | solution.py:24
  8.9 19.4 %collective-permute-start.2 = (f32[3,2,32,128]{3,2,1,0:T(8,128)}, f32[3,2,32,128]{3,2,1,0:T(8,128)S(1)}, u32[]{:S(2)}, u32[]{:S(2)}) collective-permute-start(f32[3,2,32,128]{3,2,1,0:T(8,128)} %get-tuple-element.142), channel_id=1, source_target_pairs={{0,16},{1,17},{2,18},{3,19},{4,20},{5,21},{6,22},{7,23},{8,24},{9,... | collective-permute-start | bytes 294920 | tf_op jit(solution)/shard_map/ppermute | solution.py:23
  10.2 18.1 %collective-permute-start.3 = (f32[3,2,32,128]{3,2,1,0:T(8,128)S(1)}, f32[3,2,32,128]{3,2,1,0:T(8,128)S(1)}, u32[]{:S(2)}, u32[]{:S(2)}) collective-permute-start(f32[3,2,32,128]{3,2,1,0:T(8,128)S(1)} %get-tuple-element.143), channel_id=1, source_target_pairs={{16,0},{17,1},{18,2},{19,3},{20,4},{21,5},{22,6},{23,7},{24,8},{25... | collective-permute-start | bytes 294920 | tf_op jit(solution)/shard_map/ppermute | solution.py:24
  38.0 5.9 %collective-permute-start.4 = (f32[3,2,32,128]{3,2,1,0:T(8,128)S(1)}, f32[3,2,32,128]{3,2,1,0:T(8,128)S(1)}, u32[]{:S(2)}, u32[]{:S(2)}) collective-permute-start(f32[3,2,32,128]{3,2,1,0:T(8,128)S(1)} %get-tuple-element.189), channel_id=1, source_target_pairs={{0,16},{1,17},{2,18},{3,19},{4,20},{5,21},{6,22},{7,23},{8,24},{9,... | collective-permute-start | bytes 294920 | tf_op jit(solution)/shard_map/ppermute | solution.py:23
  39.3 5.6 %collective-permute-start.5 = (f32[3,2,32,128]{3,2,1,0:T(8,128)S(1)}, f32[3,2,32,128]{3,2,1,0:T(8,128)S(1)}, u32[]{:S(2)}, u32[]{:S(2)}) collective-permute-start(f32[3,2,32,128]{3,2,1,0:T(8,128)S(1)} %get-tuple-element.190), channel_id=1, source_target_pairs={{16,0},{17,1},{18,2},{19,3},{20,4},{21,5},{22,6},{23,7},{24,8},{25... | collective-permute-start | bytes 294920 | tf_op jit(solution)/shard_map/ppermute | solution.py:24
  45.0 8.4 %collective-permute-start.6 = (f32[3,20,2,128]{3,2,1,0:T(2,128)S(1)}, f32[3,20,2,128]{3,2,1,0:T(2,128)S(1)}, u32[]{:S(2)}, u32[]{:S(2)}) collective-permute-start(f32[3,20,2,128]{3,2,1,0:T(2,128)S(1)} %get-tuple-element.160), channel_id=1, source_target_pairs={{0,1},{1,2},{2,3},{3,4},{4,5},{5,6},{6,7},{7,8},{8,9},{9,10},{10,1... | collective-permute-start | bytes 184328 | tf_op jit(solution)/shard_map/ppermute | solution.py:23
  51.3 6.4 %collective-permute-start.7 = (f32[3,20,2,128]{3,2,1,0:T(2,128)S(1)}, f32[3,20,2,128]{3,2,1,0:T(2,128)S(1)}, u32[]{:S(2)}, u32[]{:S(2)}) collective-permute-start(f32[3,20,2,128]{3,2,1,0:T(2,128)S(1)} %get-tuple-element.161), channel_id=1, source_target_pairs={{1,0},{2,1},{3,2},{4,3},{5,4},{6,5},{7,6},{8,7},{9,8},{10,9},{11,1... | collective-permute-start | bytes 184328 | tf_op jit(solution)/shard_map/ppermute | solution.py:24
  70.5 10.1 %collective-permute-start.8 = (f32[3,16,2,128]{3,2,1,0:T(2,128)S(1)}, f32[3,16,2,128]{3,2,1,0:T(2,128)S(1)}, u32[]{:S(2)}, u32[]{:S(2)}) collective-permute-start(f32[3,16,2,128]{3,2,1,0:T(2,128)S(1)} %get-tuple-element.181), channel_id=1, source_target_pairs={{0,1},{1,2},{2,3},{3,4},{4,5},{5,6},{6,7},{7,8},{8,9},{9,10},{10,1... | collective-permute-start | bytes 147464 | tf_op jit(solution)/shard_map/ppermute | solution.py:23
  72.5 8.2 %collective-permute-start.9 = (f32[3,16,2,128]{3,2,1,0:T(2,128)S(1)}, f32[3,16,2,128]{3,2,1,0:T(2,128)S(1)}, u32[]{:S(2)}, u32[]{:S(2)}) collective-permute-start(f32[3,16,2,128]{3,2,1,0:T(2,128)S(1)} %get-tuple-element.182), channel_id=1, source_target_pairs={{1,0},{2,1},{3,2},{4,3},{5,4},{6,5},{7,6},{8,7},{9,8},{10,9},{11,1... | collective-permute-start | bytes 147464 | tf_op jit(solution)/shard_map/ppermute | solution.py:24
  75.3 6.3 %collective-permute-start.10 = (f32[3,2,32,128]{3,2,1,0:T(8,128)S(1)}, f32[3,2,32,128]{3,2,1,0:T(8,128)S(1)}, u32[]{:S(2)}, u32[]{:S(2)}) collective-permute-start(f32[3,2,32,128]{3,2,1,0:T(8,128)S(1)} %get-tuple-element.186), channel_id=1, source_target_pairs={{0,16},{1,17},{2,18},{3,19},{4,20},{5,21},{6,22},{7,23},{8,24},{9,... | collective-permute-start | bytes 294920 | tf_op jit(solution)/shard_map/ppermute | solution.py:23
  76.6 5.9 %collective-permute-start.11 = (f32[3,2,32,128]{3,2,1,0:T(8,128)S(1)}, f32[3,2,32,128]{3,2,1,0:T(8,128)S(1)}, u32[]{:S(2)}, u32[]{:S(2)}) collective-permute-start(f32[3,2,32,128]{3,2,1,0:T(8,128)S(1)} %get-tuple-element.185), channel_id=1, source_target_pairs={{16,0},{17,1},{18,2},{19,3},{20,4},{21,5},{22,6},{23,7},{24,8},{25... | collective-permute-start | bytes 294920 | tf_op jit(solution)/shard_map/ppermute | solution.py:24
  84.7 6.0 %collective-permute-start.12 = (f32[3,2,32,128]{3,2,1,0:T(8,128)S(1)}, f32[3,2,32,128]{3,2,1,0:T(8,128)S(1)}, u32[]{:S(2)}, u32[]{:S(2)}) collective-permute-start(f32[3,2,32,128]{3,2,1,0:T(8,128)S(1)} %get-tuple-element.179), channel_id=1, source_target_pairs={{0,16},{1,17},{2,18},{3,19},{4,20},{5,21},{6,22},{7,23},{8,24},{9,... | collective-permute-start | bytes 294920 | tf_op jit(solution)/shard_map/ppermute | solution.py:23
  86.0 5.7 %collective-permute-start.13 = (f32[3,2,32,128]{3,2,1,0:T(8,128)S(1)}, f32[3,2,32,128]{3,2,1,0:T(8,128)S(1)}, u32[]{:S(2)}, u32[]{:S(2)}) collective-permute-start(f32[3,2,32,128]{3,2,1,0:T(8,128)S(1)} %get-tuple-element.180), channel_id=1, source_target_pairs={{16,0},{17,1},{18,2},{19,3},{20,4},{21,5},{22,6},{23,7},{24,8},{25... | collective-permute-start | bytes 294920 | tf_op jit(solution)/shard_map/ppermute | solution.py:24
  91.8 9.3 %collective-permute-start.14 = (f32[3,20,2,128]{3,2,1,0:T(2,128)S(1)}, f32[3,20,2,128]{3,2,1,0:T(2,128)S(1)}, u32[]{:S(2)}, u32[]{:S(2)}) collective-permute-start(f32[3,20,2,128]{3,2,1,0:T(2,128)S(1)} %get-tuple-element.155), channel_id=1, source_target_pairs={{0,1},{1,2},{2,3},{3,4},{4,5},{5,6},{6,7},{7,8},{8,9},{9,10},{10,1... | collective-permute-start | bytes 184328 | tf_op jit(solution)/shard_map/ppermute | solution.py:23
  97.7 6.4 %collective-permute-start.15 = (f32[3,20,2,128]{3,2,1,0:T(2,128)S(1)}, f32[3,20,2,128]{3,2,1,0:T(2,128)S(1)}, u32[]{:S(2)}, u32[]{:S(2)}) collective-permute-start(f32[3,20,2,128]{3,2,1,0:T(2,128)S(1)} %get-tuple-element.156), channel_id=1, source_target_pairs={{1,0},{2,1},{3,2},{4,3},{5,4},{6,5},{7,6},{8,7},{9,8},{10,9},{11,1... | collective-permute-start | bytes 184328 | tf_op jit(solution)/shard_map/ppermute | solution.py:24
  109.1 11.4 %collective-permute-start.16 = (f32[3,16,2,128]{3,2,1,0:T(2,128)S(1)}, f32[3,16,2,128]{3,2,1,0:T(2,128)S(1)}, u32[]{:S(2)}, u32[]{:S(2)}) collective-permute-start(f32[3,16,2,128]{3,2,1,0:T(2,128)S(1)} %get-tuple-element.171), channel_id=1, source_target_pairs={{0,1},{1,2},{2,3},{3,4},{4,5},{5,6},{6,7},{7,8},{8,9},{9,10},{10,1... | collective-permute-start | bytes 147464 | tf_op jit(solution)/shard_map/ppermute | solution.py:23
  111.0 9.5 %collective-permute-start.17 = (f32[3,16,2,128]{3,2,1,0:T(2,128)S(1)}, f32[3,16,2,128]{3,2,1,0:T(2,128)S(1)}, u32[]{:S(2)}, u32[]{:S(2)}) collective-permute-start(f32[3,16,2,128]{3,2,1,0:T(2,128)S(1)} %get-tuple-element.172), channel_id=1, source_target_pairs={{1,0},{2,1},{3,2},{4,3},{5,4},{6,5},{7,6},{8,7},{9,8},{10,9},{11,1... | collective-permute-start | bytes 147464 | tf_op jit(solution)/shard_map/ppermute | solution.py:24
  115.1 6.3 %collective-permute-start.18 = (f32[3,2,32,128]{3,2,1,0:T(8,128)S(1)}, f32[3,2,32,128]{3,2,1,0:T(8,128)S(1)}, u32[]{:S(2)}, u32[]{:S(2)}) collective-permute-start(f32[3,2,32,128]{3,2,1,0:T(8,128)S(1)} %get-tuple-element.176), channel_id=1, source_target_pairs={{0,16},{1,17},{2,18},{3,19},{4,20},{5,21},{6,22},{7,23},{8,24},{9,... | collective-permute-start | bytes 294920 | tf_op jit(solution)/shard_map/ppermute | solution.py:23
  116.4 5.9 %collective-permute-start.19 = (f32[3,2,32,128]{3,2,1,0:T(8,128)S(1)}, f32[3,2,32,128]{3,2,1,0:T(8,128)S(1)}, u32[]{:S(2)}, u32[]{:S(2)}) collective-permute-start(f32[3,2,32,128]{3,2,1,0:T(8,128)S(1)} %get-tuple-element.175), channel_id=1, source_target_pairs={{16,0},{17,1},{18,2},{19,3},{20,4},{21,5},{22,6},{23,7},{24,8},{25... | collective-permute-start | bytes 294920 | tf_op jit(solution)/shard_map/ppermute | solution.py:24
  190.1 8.3 %collective-permute-start.24 = (f32[2,128,1]{1,2,0:T(1,128)S(1)}, f32[2,128,1]{1,2,0:T(1,128)S(1)}, u32[]{:S(2)}, u32[]{:S(2)}) collective-permute-start(f32[2,128,1]{1,2,0:T(1,128)S(1)} %pad_maximum_fusion.64), channel_id=1, source_target_pairs={{1,0},{2,1},{3,2},{4,3},{5,4},{6,5},{7,6},{8,7},{9,8},{10,9},{11,1... | collective-permute-start | bytes 3080 | tf_op jit(solution)/shard_map/ppermute | solution.py:37
  194.8 4.4 %collective-permute-start.26 = (f32[2,1,256]{2,1,0:T(1,128)S(1)}, f32[2,1,256]{2,1,0:T(1,128)S(1)}, u32[]{:S(2)}, u32[]{:S(2)}) collective-permute-start(f32[2,1,256]{2,1,0:T(1,128)S(1)} %pad_maximum_fusion.63), channel_id=1, source_target_pairs={{16,0},{17,1},{18,2},{19,3},{20,4},{21,5},{22,6},{23,7},{24,8},{25... | collective-permute-start | bytes 6152 | tf_op jit(solution)/shard_map/ppermute | solution.py:37
  200.7 5.9 %collective-permute-start.25 = (f32[128,1]{1,0:T(8,128)S(1)}, f32[128,1]{1,0:T(8,128)S(1)}, u32[]{:S(2)}, u32[]{:S(2)}) collective-permute-start(f32[128,1]{1,0:T(8,128)S(1)} %slice.2012), channel_id=1, source_target_pairs={{0,1},{1,2},{2,3},{3,4},{4,5},{5,6},{6,7},{7,8},{8,9},{9,10},{10,1... | collective-permute-start | bytes 1544 | tf_op jit(solution)/shard_map/ppermute | solution.py:37
  205.2 4.3 %collective-permute-start.27 = (f32[1,256]{1,0:T(1,128)S(1)}, f32[1,256]{1,0:T(1,128)S(1)}, u32[]{:S(2)}, u32[]{:S(2)}) collective-permute-start(f32[1,256]{1,0:T(1,128)S(1)} %slice.2020), channel_id=1, source_target_pairs={{0,16},{1,17},{2,18},{3,19},{4,20},{5,21},{6,22},{7,23},{8,24},{9,... | collective-permute-start | bytes 3080 | tf_op jit(solution)/shard_map/ppermute | solution.py:37
  210.6 9.6 %collective-permute-start.28 = (f32[128,1]{1,0:T(8,128)S(1)}, f32[128,1]{1,0:T(8,128)S(1)}, u32[]{:S(2)}, u32[]{:S(2)}) collective-permute-start(f32[128,1]{1,0:T(8,128)S(1)} %slice.2024), channel_id=1, source_target_pairs={{1,0},{2,1},{3,2},{4,3},{5,4},{6,5},{7,6},{8,7},{9,8},{10,9},{11,1... | collective-permute-start | bytes 1544 | tf_op jit(solution)/shard_map/ppermute | solution.py:37
  212.7 7.6 %collective-permute-start.30 = (f32[1,256]{1,0:T(1,128)S(1)}, f32[1,256]{1,0:T(1,128)S(1)}, u32[]{:S(2)}, u32[]{:S(2)}) collective-permute-start(f32[1,256]{1,0:T(1,128)S(1)} %slice.2028), channel_id=1, source_target_pairs={{16,0},{17,1},{18,2},{19,3},{20,4},{21,5},{22,6},{23,7},{24,8},{25... | collective-permute-start | bytes 3080 | tf_op jit(solution)/shard_map/ppermute | solution.py:37
  214.8 17.1 %collective-permute-start.20 = (f32[3,2,32,128]{3,2,1,0:T(8,128)S(1)}, f32[3,2,32,128]{3,2,1,0:T(8,128)S(1)}, u32[]{:S(2)}, u32[]{:S(2)}) collective-permute-start(f32[3,2,32,128]{3,2,1,0:T(8,128)S(1)} %get-tuple-element.169), channel_id=1, source_target_pairs={{0,16},{1,17},{2,18},{3,19},{4,20},{5,21},{6,22},{7,23},{8,24},{9,... | collective-permute-start | bytes 294920 | tf_op jit(solution)/shard_map/ppermute | solution.py:23
  216.1 15.8 %collective-permute-start.21 = (f32[3,2,32,128]{3,2,1,0:T(8,128)S(1)}, f32[3,2,32,128]{3,2,1,0:T(8,128)S(1)}, u32[]{:S(2)}, u32[]{:S(2)}) collective-permute-start(f32[3,2,32,128]{3,2,1,0:T(8,128)S(1)} %get-tuple-element.170), channel_id=1, source_target_pairs={{16,0},{17,1},{18,2},{19,3},{20,4},{21,5},{22,6},{23,7},{24,8},{25... | collective-permute-start | bytes 294920 | tf_op jit(solution)/shard_map/ppermute | solution.py:24
  220.5 7.4 %collective-permute-start.29 = (f32[128,1]{1,0:T(8,128)S(1)}, f32[128,1]{1,0:T(8,128)S(1)}, u32[]{:S(2)}, u32[]{:S(2)}) collective-permute-start(f32[128,1]{1,0:T(8,128)S(1)} %slice.2025), channel_id=1, source_target_pairs={{0,1},{1,2},{2,3},{3,4},{4,5},{5,6},{6,7},{7,8},{8,9},{9,10},{10,1... | collective-permute-start | bytes 1544 | tf_op jit(solution)/shard_map/ppermute | solution.py:37
  225.8 4.3 %collective-permute-start.31 = (f32[1,256]{1,0:T(1,128)S(1)}, f32[1,256]{1,0:T(1,128)S(1)}, u32[]{:S(2)}, u32[]{:S(2)}) collective-permute-start(f32[1,256]{1,0:T(1,128)S(1)} %slice.2029), channel_id=1, source_target_pairs={{0,16},{1,17},{2,18},{3,19},{4,20},{5,21},{6,22},{7,23},{8,24},{9,... | collective-permute-start | bytes 3080 | tf_op jit(solution)/shard_map/ppermute | solution.py:37
  231.9 5.5 %collective-permute-start.22 = (f32[3,20,2,128]{3,2,1,0:T(2,128)S(1)}, f32[3,20,2,128]{3,2,1,0:T(2,128)S(1)}, u32[]{:S(2)}, u32[]{:S(2)}) collective-permute-start(f32[3,20,2,128]{3,2,1,0:T(2,128)S(1)} %get-tuple-element.150), channel_id=1, source_target_pairs={{0,1},{1,2},{2,3},{3,4},{4,5},{5,6},{6,7},{7,8},{8,9},{9,10},{10,1... | collective-permute-start | bytes 184328 | tf_op jit(solution)/shard_map/ppermute | solution.py:23
  235.0 6.6 %collective-permute-start.23 = (f32[3,20,2,128]{3,2,1,0:T(2,128)S(1)}, f32[3,20,2,128]{3,2,1,0:T(2,128)S(1)}, u32[]{:S(2)}, u32[]{:S(2)}) collective-permute-start(f32[3,20,2,128]{3,2,1,0:T(2,128)S(1)} %get-tuple-element.151), channel_id=1, source_target_pairs={{1,0},{2,1},{3,2},{4,3},{5,4},{6,5},{7,6},{8,7},{9,8},{10,9},{11,1... | collective-permute-start | bytes 184328 | tf_op jit(solution)/shard_map/ppermute | solution.py:24
  (61 other events, 326.4 us)
